TPU v7x, 256 devices: a whole 4x4x8 slice. The times are simulated.
256 devices in a mesh: op: 16 (over x_lo, y, core), sec: 16 (over x_hi, z).
Axes of the slice: x: 4 (x_hi: 2, x_lo: 2; x = x_hi * 2 + x_lo), y: 4, z: 8, core: 2. Of those that a mesh axis runs over, the one named last changes fastest.
Arguments:
- psi: bfloat16 [16, 512, 512], P('sec'), may hold values from -6 to 6
- left_env: bfloat16 [128, 16, 512, 512], P('op', 'sec'), may hold values from -0.375 to 0.375
- right_env: bfloat16 [128, 16, 512, 512], P('op', 'sec'), may hold values from -0.25 to 0.25
- pair_code: int32 [128], P('op'), may hold values from 0 to 2
- sketch: bfloat16 [16, 512, 128], P('sec'), may hold values from -0.25 to 0.25
Outputs:
- sigma: bfloat16 [512, 8192], P('op', 'sec')
- basis: float32 [512, 2048], P('op', 'sec')
All inputs are finite; a program needn't handle non-finite values.
Results may differ from a plain program's by a relative error of at most 0.0055.
Values may be sent and summed in bfloat16 or wider, within the bound.
No kernel may reach another device: no remote copies, remote signals or barrier semaphores. Data moves between devices by JAX's collectives and lax.ppermute only.
A program may use at most 64 MiB of HBM per device.

v0:
```python
import math
import jax
import jax.numpy as jnp
from jax import lax
from jax.sharding import PartitionSpec as P


def padded_2(block, sides, width):
    for axis, dim in sides:
        count = lax.axis_size(axis)
        forward = [(i, i + 1) for i in range(count - 1)]
        backward = [(target, source) for source, target in forward]
        low = lax.ppermute(
            lax.slice_in_dim(block, block.shape[dim] - width, None, axis=dim), axis, forward
        )
        high = lax.ppermute(lax.slice_in_dim(block, 0, width, axis=dim), axis, backward)
        block = jnp.concatenate([low, block, high], axis=dim)
    return block


def range_basis(sigma_rows, sketch, width):
    count = sigma_rows.shape[0]
    sec_dev = sketch.shape[0]
    sampled = jnp.einsum(
        "ajd,jdk->jak",
        sigma_rows.reshape(count, sec_dev, width),
        sketch,
        preferred_element_type=jnp.float32,
    )
    return sampled


def finish_basis(sampled, gram, width):
    lower = jnp.linalg.cholesky(gram)
    solved = lax.linalg.triangular_solve(
        lower, sampled, left_side=False, lower=True, transpose_a=True
    )
    sec_dev, count, cols = solved.shape
    return math.sqrt(width) * solved.transpose(1, 0, 2).reshape(count, sec_dev * cols)


def body(psi, left_env, right_env, pair_code, sketch):
    t_dev, sec_dev, width, unused = left_env.shape
    n_op = lax.axis_size("op")
    rows = width // n_op
    scale = 1.0 / math.sqrt(t_dev * n_op)
    padded = padded_2(psi, (("sec", 0),), 1)

    def one_term(index, total):
        code = pair_code[index]
        source = lax.dynamic_slice_in_dim(padded, 2 - code, sec_dev, 0)
        left_rows = left_env[index]
        inner = jnp.einsum(
            "jab,jbc->jac", left_rows, source, preferred_element_type=jnp.float32
        ).astype(jnp.bfloat16)
        return total + scale * jnp.einsum(
            "jac,jcd->jad", inner, right_env[index], preferred_element_type=jnp.float32
        )

    total = lax.fori_loop(
        0, t_dev, one_term, jnp.zeros((sec_dev, lax.axis_size("op") * rows, width), jnp.float32)
    )
    summed = lax.psum_scatter(
        total.transpose(1, 0, 2).reshape(lax.axis_size("op") * rows, sec_dev * width),
        "op",
        scatter_dimension=0,
        tiled=True,
    )
    sigma_rows = summed.astype(jnp.bfloat16)
    sampled = range_basis(sigma_rows, sketch, width)
    gram_part = jnp.einsum("jak,jal->jkl", sampled, sampled, precision=lax.Precision.HIGHEST)
    gram = lax.psum(gram_part, "op")
    basis = finish_basis(sampled, gram, width)
    return (sigma_rows, basis)


def solution(mesh):
    in_specs = (
        P("sec", None, None),
        P("op", "sec", None, None),
        P("op", "sec", None, None),
        P("op"),
        P("sec", None, None),
    )
    out_specs = (P("op", "sec"), P("op", "sec"))
    return jax.shard_map(body, mesh=mesh, in_specs=in_specs, out_specs=out_specs, check_vma=False)
```

profile of v0, /device:TPU:25, one launch (start us, length us, event | category | flops | bytes accessed | tf_op | source)
XLA Modules:
  0.0 275.1 jit_solution(13141491743284272402)
XLA Ops:
  7.2 3.6 %collective-permute-start = (bf16[1,512,512]{2,1,0:T(8,128)(2,1)}, bf16[1,512,512]{2,1,0:T(8,128)(2,1)S(1)}, u32[]{:S(2)}, u32[]{:S(2)}) collective-permute-start(bf16[1,512,512]{2,1,0:T(8,128)(2,1)} %param.7), channel_id=1, source_target_pairs={{0,1},{1,2},{2,3},{3,4},{4,5},{5,6},{6,7},{7,8},{8,9},{9,10},{10,1... | collective-permute-start | bytes 1572872 | tf_op jit(solution)/shard_map/ppermute | solution.py:13
  10.8 1.3 collective-permute-start.1
  12.1 9.6 %collective-permute-done = bf16[1,512,512]{2,1,0:T(8,128)(2,1)S(1)} collective-permute-done((bf16[1,512,512]{2,1,0:T(8,128)(2,1)}, bf16[1,512,512]{2,1,0:T(8,128)(2,1)S(1)}, u32[]{:S(2)}, u32[]{:S(2)}) %collective-permute-start) | collective-permute-done | bytes 524320 | tf_op jit(solution)/shard_map/ppermute | solution.py:13
  21.7 4.2 %collective-permute-done.1 = bf16[1,512,512]{2,1,0:T(8,128)(2,1)} collective-permute-done((bf16[1,512,512]{2,1,0:T(8,128)(2,1)}, bf16[1,512,512]{2,1,0:T(8,128)(2,1)}, u32[]{:S(2)}, u32[]{:S(2)}) %collective-permute-start.1) | collective-permute-done | bytes 524320 | tf_op jit(solution)/shard_map/ppermute | solution.py:16
  25.9 1.4 pad_maximum_fusion
  27.2 31.5 %while.16 = (s32[]{:T(128)}, f32[1,512,512]{2,1,0:T(8,128)S(1)}, bf16[8,1,512,512]{3,2,1,0:T(8,128)(2,1)}, s32[8]{0:T(128)S(1)}, bf16[3,512,512]{2,1,0:T(8,128)(...) while((s32[]{:T(128)}, f32[1,512,512]{2,1,0:T(8,128)S(1)}, ...), condition=%wide.region_1.0_spmd.clone, body=%wide.region_0.0_spmd.clone.sunk | while | flops 537919488 | bytes 3671213 | solution.py:60
  27.3 0.6 dynamic_slice.65
  29.1 2.0 fusion.30
  31.2 0.6 dynamic_slice.65
  33.1 2.0 fusion.30
  35.1 0.6 dynamic_slice.65
  37.0 2.0 fusion.30
  39.1 0.6 dynamic_slice.65
  41.0 2.0 fusion.30
  43.0 0.6 dynamic_slice.65
  44.9 2.0 fusion.30
  48.8 2.0 fusion.30
  50.9 0.6 dynamic_slice.65
  52.8 2.0 fusion.30
  56.7 2.0 fusion.30
  58.8 1.0 copy-done.1
  59.8 66.4 %reduce-scatter.2.cloned.1.call-done = f32[32,512]{1,0:T(8,128)} async-done(((f32[512,512]{1,0:T(8,128)}), f32[32,512]{1,0:T(8,128)}) %reduce-scatter.2.cloned.1.call-update) | async-done | bytes 65552 | tf_op jit(solution)/shard_map/reduce_scatter | solution.py:63
  126.2 0.8 convert_element_type.14
  127.2 0.9 convolution_bitcast_fusion
  128.2 114.6 %all-reduce.2.cloned.1.call-done = f32[1,128,128]{1,2,0:T(8,128)} async-done(((f32[1,128,128]{1,2,0:T(8,128)}), f32[1,128,128]{1,2,0:T(8,128)}) %all-reduce.2.cloned.1.call-update) | async-done | bytes 65552 | tf_op jit(solution)/shard_map/psum | solution.py:72
  242.8 0.9 copy.8
  243.7 0.9 fusion.18
  244.6 11.7 %custom-call.7 = f32[1,128,128]{2,1,0:T(8,128)S(1)} custom-call(f32[1,128,128]{2,1,0:T(8,128)S(1)} %fusion.18), custom_call_target="Cholesky" | custom-call | tf_op jit(solution)/shard_map/jit(cholesky)/cholesky | solution.py:34
  256.3 0.6 compare_reduce_fusion
  256.9 0.7 fusion.16
  257.6 9.8 %custom-call.8 = f32[1,1,128,128]{2,3,1,0:T(8,128)S(1)} custom-call(f32[1,1,128,128]{3,2,1,0:T(8,128)S(1)} %fusion.16), custom_call_target="InvertDiagBlocksLowerTriangular" | custom-call | tf_op jit(solution)/shard_map/triangular_solve | solution.py:35
  267.4 0.8 convolution_multiply_fusion.1
  (16 shorter events, 1.5 us)
Async XLA Ops:
  7.2 119.9 %copy-start = (bf16[1,512,128]{2,1,0:T(8,128)(2,1)S(1)}, bf16[1,512,128]{2,1,0:T(8,128)(2,1)}, u32[]{:S(2)}) copy-start(bf16[1,512,128]{2,1,0:T(8,128)(2,1)} %param.11) | copy-start | bytes 393220
  7.2 119.1 %reduce-scatter.2.cloned.1.call-start = ((), (), s32[]{:S(2)}) async-start(), calls=%async_computation.1 | async-start | bytes 1114112 | tf_op jit(solution)/shard_map/reduce_scatter | solution.py:63
  7.2 14.5 %collective-permute-start = (bf16[1,512,512]{2,1,0:T(8,128)(2,1)}, bf16[1,512,512]{2,1,0:T(8,128)(2,1)S(1)}, u32[]{:S(2)}, u32[]{:S(2)}) collective-permute-start(bf16[1,512,512]{2,1,0:T(8,128)(2,1)} %param.7), channel_id=1, source_target_pairs={{0,1},{1,2},{2,3},{3,4},{4,5},{5,6},{6,7},{7,8},{8,9},{9,10},{10,1... | collective-permute-start | bytes 1572872 | tf_op jit(solution)/shard_map/ppermute | solution.py:13
  10.8 15.1 %collective-permute-start.1 = (bf16[1,512,512]{2,1,0:T(8,128)(2,1)}, bf16[1,512,512]{2,1,0:T(8,128)(2,1)}, u32[]{:S(2)}, u32[]{:S(2)}) collective-permute-start(bf16[1,512,512]{2,1,0:T(8,128)(2,1)} %param.7), channel_id=1, source_target_pairs={{1,0},{2,1},{3,2},{4,3},{5,4},{6,5},{7,6},{8,7},{9,8},{10,9},{11,1... | collective-permute-start | bytes 1572872 | tf_op jit(solution)/shard_map/ppermute | solution.py:16
  12.1 15.1 %copy-start.3 = (s32[8]{0:T(128)S(1)}, s32[8]{0:T(128)}, u32[]{:S(2)}) copy-start(s32[8]{0:T(128)} %param.10) | copy-start | bytes 100
  58.7 1.0 copy-start.1
  59.7 183.0 %all-reduce.2.cloned.1.call-start = ((), (), s32[]{:S(2)}) async-start(), calls=%async_computation.2 | async-start | bytes 131072 | tf_op jit(solution)/shard_map/psum | solution.py:72
  127.1 141.1 %copy-start.2 = (bf16[32,512]{1,0:T(8,128)(2,1)}, bf16[32,512]{1,0:T(8,128)(2,1)S(1)}, u32[]{:S(2)}) copy-start(bf16[32,512]{1,0:T(8,128)(2,1)S(1)} %convert_element_type.14) | copy-start | bytes 98308
Sparse Core Ops, SparseCore 0:
  59.9 66.3 reduce-scatter.1
  128.9 113.8 all-reduce.1
where the time goes:
time: 276 us; the launch traced here: 275 us
  waiting for transfers between devices  195 us (71%)
  other arithmetic  25.9 us (9%)
  matrix products  18 us (7%)
  between operations  14.1 us (5%)
  loops' own time  10.6 us (4%)
  local copies, waits for them, and re-layouts  6.61 us (2%)
  starting transfers between devices  4.95 us (2%)
    psum x1, waiting for transfers between devices, body(): gram = lax.psum(gram_part, 'op')  115 us
    reduce_scatter x1, waiting for transfers between devices, body(): lax.psum_scatter(total.transpose(1, 0, 2).reshape(lax.axis_size('op') * r...  66.4 us
    dot_general x8, matrix products, one_term(): jnp.einsum('jac,jcd->jad', inner, right_env[index], preferred_element_typ...  16.2 us
    another operation x3, other arithmetic, finish_basis(): lower = jnp.linalg.cholesky(gram)  12.4 us
    another operation x1, loops' own time, body(): lax.fori_loop(0, t_dev, one_term, jnp.zeros((sec_dev, lax.axis_size('op')...  10.6 us
    another operation x2, other arithmetic, finish_basis(): lax.linalg.triangular_solve(lower, sampled, left_side=False, lower=True,...  10.5 us
    ppermute x1, waiting for transfers between devices, padded_2(): lax.ppermute(lax.slice_in_dim(block, block.shape[dim] - width, None, axis...  9.55 us
  transfers between devices with their start and end apart: 4, of which 4 were waited for; matrix products, arithmetic and copies ran while one was open for 0% of the time, Pallas kernels for 0%

commit v1 on v0

--- a/solution.py
+++ b/solution.py
@@ -69,7 +69,7 @@
     sigma_rows = summed.astype(jnp.bfloat16)
     sampled = range_basis(sigma_rows, sketch, width)
     gram_part = jnp.einsum("jak,jal->jkl", sampled, sampled, precision=lax.Precision.HIGHEST)
-    gram = lax.psum(gram_part, "op")
+    gram = jnp.sum(lax.all_gather(gram_part, "op"), axis=0)
     basis = finish_basis(sampled, gram, width)
     return (sigma_rows, basis)
 

time: 276 us -> 197 us (0.71)
  waiting for transfers between devices: 195 us -> 115 us
    psum x1 -> x0, waiting for transfers between devices: 115 us -> none  [body(): gram = lax.psum(gram_part, 'op')]
    all_gather x0 -> x1, waiting for transfers between devices: none -> 34.5 us  [body(): gram = jnp.sum(lax.all_gather(gram_part, 'op'), axis=0)]
where the time goes in v1:
time: 197 us; the launch traced here: 195 us
  waiting for transfers between devices  115 us (58%)
  other arithmetic  26.4 us (13%)
  matrix products  18 us (9%)
  between operations  14.2 us (7%)
  loops' own time  10.6 us (5%)
  local copies, waits for them, and re-layouts  5.86 us (3%)
  starting transfers between devices  4.95 us (3%)
    reduce_scatter x1, waiting for transfers between devices, body(): lax.psum_scatter(total.transpose(1, 0, 2).reshape(lax.axis_size('op') * r...  66.4 us
    all_gather x1, waiting for transfers between devices, body(): gram = jnp.sum(lax.all_gather(gram_part, 'op'), axis=0)  34.5 us
    dot_general x8, matrix products, one_term(): jnp.einsum('jac,jcd->jad', inner, right_env[index], preferred_element_typ...  16.2 us
    another operation x3, other arithmetic, finish_basis(): lower = jnp.linalg.cholesky(gram)  12.4 us
    another operation x1, loops' own time, body(): lax.fori_loop(0, t_dev, one_term, jnp.zeros((sec_dev, lax.axis_size('op')...  10.6 us
    another operation x2, other arithmetic, finish_basis(): lax.linalg.triangular_solve(lower, sampled, left_side=False, lower=True,...  10.5 us
    ppermute x1, waiting for transfers between devices, padded_2(): lax.ppermute(lax.slice_in_dim(block, block.shape[dim] - width, None, axis...  9.55 us
    dynamic_slice x8, local copies, waits for them, and re-layouts, one_term(): code = pair_code[index]  4.69 us
  transfers between devices with their start and end apart: 4, of which 4 were waited for; matrix products, arithmetic and copies ran while one was open for 0% of the time, Pallas kernels for 0%

profile of v1, /device:TPU:25, one launch (start us, length us, event | category | flops | bytes accessed | tf_op | source)
XLA Modules:
  0.0 194.7 jit_solution(10923980764812404299)
XLA Ops:
  7.2 3.6 %collective-permute-start = (bf16[1,512,512]{2,1,0:T(8,128)(2,1)}, bf16[1,512,512]{2,1,0:T(8,128)(2,1)S(1)}, u32[]{:S(2)}, u32[]{:S(2)}) collective-permute-start(bf16[1,512,512]{2,1,0:T(8,128)(2,1)} %param.7), channel_id=1, source_target_pairs={{0,1},{1,2},{2,3},{3,4},{4,5},{5,6},{6,7},{7,8},{8,9},{9,10},{10,1... | collective-permute-start | bytes 1572872 | tf_op jit(solution)/shard_map/ppermute | solution.py:13
  10.8 1.3 collective-permute-start.1
  12.1 9.6 %collective-permute-done = bf16[1,512,512]{2,1,0:T(8,128)(2,1)S(1)} collective-permute-done((bf16[1,512,512]{2,1,0:T(8,128)(2,1)}, bf16[1,512,512]{2,1,0:T(8,128)(2,1)S(1)}, u32[]{:S(2)}, u32[]{:S(2)}) %collective-permute-start) | collective-permute-done | bytes 524320 | tf_op jit(solution)/shard_map/ppermute | solution.py:13
  21.7 4.2 %collective-permute-done.1 = bf16[1,512,512]{2,1,0:T(8,128)(2,1)} collective-permute-done((bf16[1,512,512]{2,1,0:T(8,128)(2,1)}, bf16[1,512,512]{2,1,0:T(8,128)(2,1)}, u32[]{:S(2)}, u32[]{:S(2)}) %collective-permute-start.1) | collective-permute-done | bytes 524320 | tf_op jit(solution)/shard_map/ppermute | solution.py:16
  25.9 1.4 pad_maximum_fusion
  27.2 31.5 %while.16 = (s32[]{:T(128)}, f32[1,512,512]{2,1,0:T(8,128)S(1)}, bf16[8,1,512,512]{3,2,1,0:T(8,128)(2,1)}, s32[8]{0:T(128)S(1)}, bf16[3,512,512]{2,1,0:T(8,128)(...) while((s32[]{:T(128)}, f32[1,512,512]{2,1,0:T(8,128)S(1)}, ...), condition=%wide.region_1.0_spmd.clone, body=%wide.region_0.0_spmd.clone.sunk | while | flops 537919488 | bytes 3671213 | solution.py:60
  27.3 0.6 dynamic_slice.65
  29.1 2.0 %fusion.31 = f32[1,512,512]{2,1,0:T(8,128)S(1)} fusion(f32[1,512,512]{2,1,0:T(8,128)S(1)} %get-tuple-element.238, bf16[8,1,512,512]{3,2,1,0:T(8,128)(2,1)} %get-tuple-element.252, s32[]{:T(128)} %get-tuple-element.237, bf16[3,512,512]{2,1,0:T(8,128)(2,1)S(1)} %get-tuple-element.251, s32[]{:T(128)S(6)} %select_n.30, ...), kind=kOutput, calls=%fused_computation.2.clone.1 | convolution fusion | flops 537919488 | bytes 3671045 | tf_op jit(solution)/shard_map/while/body/eval_jaxpr/jac,jcd->jad/dot_general | solution.py:56
  31.2 0.6 dynamic_slice.65
  33.1 2.0 %fusion.31 = f32[1,512,512]{2,1,0:T(8,128)S(1)} fusion(f32[1,512,512]{2,1,0:T(8,128)S(1)} %get-tuple-element.238, bf16[8,1,512,512]{3,2,1,0:T(8,128)(2,1)} %get-tuple-element.252, s32[]{:T(128)} %get-tuple-element.237, bf16[3,512,512]{2,1,0:T(8,128)(2,1)S(1)} %get-tuple-element.251, s32[]{:T(128)S(6)} %select_n.30, ...), kind=kOutput, calls=%fused_computation.2.clone.1 | convolution fusion | flops 537919488 | bytes 3671045 | tf_op jit(solution)/shard_map/while/body/eval_jaxpr/jac,jcd->jad/dot_general | solution.py:56
  35.1 0.6 dynamic_slice.65
  37.0 2.0 %fusion.31 = f32[1,512,512]{2,1,0:T(8,128)S(1)} fusion(f32[1,512,512]{2,1,0:T(8,128)S(1)} %get-tuple-element.238, bf16[8,1,512,512]{3,2,1,0:T(8,128)(2,1)} %get-tuple-element.252, s32[]{:T(128)} %get-tuple-element.237, bf16[3,512,512]{2,1,0:T(8,128)(2,1)S(1)} %get-tuple-element.251, s32[]{:T(128)S(6)} %select_n.30, ...), kind=kOutput, calls=%fused_computation.2.clone.1 | convolution fusion | flops 537919488 | bytes 3671045 | tf_op jit(solution)/shard_map/while/body/eval_jaxpr/jac,jcd->jad/dot_general | solution.py:56
  39.1 0.6 dynamic_slice.65
  41.0 2.0 %fusion.31 = f32[1,512,512]{2,1,0:T(8,128)S(1)} fusion(f32[1,512,512]{2,1,0:T(8,128)S(1)} %get-tuple-element.238, bf16[8,1,512,512]{3,2,1,0:T(8,128)(2,1)} %get-tuple-element.252, s32[]{:T(128)} %get-tuple-element.237, bf16[3,512,512]{2,1,0:T(8,128)(2,1)S(1)} %get-tuple-element.251, s32[]{:T(128)S(6)} %select_n.30, ...), kind=kOutput, calls=%fused_computation.2.clone.1 | convolution fusion | flops 537919488 | bytes 3671045 | tf_op jit(solution)/shard_map/while/body/eval_jaxpr/jac,jcd->jad/dot_general | solution.py:56
  43.0 0.6 dynamic_slice.65
  44.9 2.0 %fusion.31 = f32[1,512,512]{2,1,0:T(8,128)S(1)} fusion(f32[1,512,512]{2,1,0:T(8,128)S(1)} %get-tuple-element.238, bf16[8,1,512,512]{3,2,1,0:T(8,128)(2,1)} %get-tuple-element.252, s32[]{:T(128)} %get-tuple-element.237, bf16[3,512,512]{2,1,0:T(8,128)(2,1)S(1)} %get-tuple-element.251, s32[]{:T(128)S(6)} %select_n.30, ...), kind=kOutput, calls=%fused_computation.2.clone.1 | convolution fusion | flops 537919488 | bytes 3671045 | tf_op jit(solution)/shard_map/while/body/eval_jaxpr/jac,jcd->jad/dot_general | solution.py:56
  46.9 0.6 dynamic_slice.65
  48.8 2.0 %fusion.31 = f32[1,512,512]{2,1,0:T(8,128)S(1)} fusion(f32[1,512,512]{2,1,0:T(8,128)S(1)} %get-tuple-element.238, bf16[8,1,512,512]{3,2,1,0:T(8,128)(2,1)} %get-tuple-element.252, s32[]{:T(128)} %get-tuple-element.237, bf16[3,512,512]{2,1,0:T(8,128)(2,1)S(1)} %get-tuple-element.251, s32[]{:T(128)S(6)} %select_n.30, ...), kind=kOutput, calls=%fused_computation.2.clone.1 | convolution fusion | flops 537919488 | bytes 3671045 | tf_op jit(solution)/shard_map/while/body/eval_jaxpr/jac,jcd->jad/dot_general | solution.py:56
  50.9 0.6 dynamic_slice.65
  52.8 2.0 %fusion.31 = f32[1,512,512]{2,1,0:T(8,128)S(1)} fusion(f32[1,512,512]{2,1,0:T(8,128)S(1)} %get-tuple-element.238, bf16[8,1,512,512]{3,2,1,0:T(8,128)(2,1)} %get-tuple-element.252, s32[]{:T(128)} %get-tuple-element.237, bf16[3,512,512]{2,1,0:T(8,128)(2,1)S(1)} %get-tuple-element.251, s32[]{:T(128)S(6)} %select_n.30, ...), kind=kOutput, calls=%fused_computation.2.clone.1 | convolution fusion | flops 537919488 | bytes 3671045 | tf_op jit(solution)/shard_map/while/body/eval_jaxpr/jac,jcd->jad/dot_general | solution.py:56
  56.7 2.0 %fusion.31 = f32[1,512,512]{2,1,0:T(8,128)S(1)} fusion(f32[1,512,512]{2,1,0:T(8,128)S(1)} %get-tuple-element.238, bf16[8,1,512,512]{3,2,1,0:T(8,128)(2,1)} %get-tuple-element.252, s32[]{:T(128)} %get-tuple-element.237, bf16[3,512,512]{2,1,0:T(8,128)(2,1)S(1)} %get-tuple-element.251, s32[]{:T(128)S(6)} %select_n.30, ...), kind=kOutput, calls=%fused_computation.2.clone.1 | convolution fusion | flops 537919488 | bytes 3671045 | tf_op jit(solution)/shard_map/while/body/eval_jaxpr/jac,jcd->jad/dot_general | solution.py:56
  58.8 1.0 copy-done.1
  59.8 66.4 %reduce-scatter.2.cloned.1.call-done = f32[32,512]{1,0:T(8,128)} async-done(((f32[512,512]{1,0:T(8,128)}), f32[32,512]{1,0:T(8,128)}) %reduce-scatter.2.cloned.1.call-update) | async-done | bytes 65552 | tf_op jit(solution)/shard_map/reduce_scatter | solution.py:63
  126.2 0.8 convert_element_type.14
  127.2 0.9 fusion.19
  128.2 34.5 %all-gather.3.cloned.1.call-done = f32[2048,128]{1,0:T(8,128)} async-done(((f32[128,128]{1,0:T(8,128)}), f32[2048,128]{1,0:T(8,128)}) %all-gather.3.cloned.1.call-update) | async-done | bytes 1048592 | tf_op jit(solution)/shard_map/all_gather | solution.py:72
  162.7 1.3 reduce.10
  164.2 11.7 %custom-call.7 = f32[1,128,128]{2,1,0:T(8,128)S(1)} custom-call(f32[1,128,128]{2,1,0:T(8,128)S(1)} %fusion.17), custom_call_target="Cholesky" | custom-call | tf_op jit(solution)/shard_map/jit(cholesky)/cholesky | solution.py:34
  175.9 0.6 compare_reduce_fusion
  176.6 0.7 fusion.16
  177.3 9.8 %custom-call.8 = f32[1,1,128,128]{2,3,1,0:T(8,128)S(1)} custom-call(f32[1,1,128,128]{3,2,1,0:T(8,128)S(1)} %fusion.16), custom_call_target="InvertDiagBlocksLowerTriangular" | custom-call | tf_op jit(solution)/shard_map/triangular_solve | solution.py:35
  187.1 0.8 convolution_multiply_fusion.1
  (18 shorter events, 1.1 us)
Async XLA Ops:
  7.2 119.9 %copy-start = (bf16[1,512,128]{2,1,0:T(8,128)(2,1)S(1)}, bf16[1,512,128]{2,1,0:T(8,128)(2,1)}, u32[]{:S(2)}) copy-start(bf16[1,512,128]{2,1,0:T(8,128)(2,1)} %param.11) | copy-start | bytes 393220
  7.2 119.1 %reduce-scatter.2.cloned.1.call-start = ((), (), s32[]{:S(2)}) async-start(), calls=%async_computation.1 | async-start | bytes 1114112 | tf_op jit(solution)/shard_map/reduce_scatter | solution.py:63
  7.2 14.5 %collective-permute-start = (bf16[1,512,512]{2,1,0:T(8,128)(2,1)}, bf16[1,512,512]{2,1,0:T(8,128)(2,1)S(1)}, u32[]{:S(2)}, u32[]{:S(2)}) collective-permute-start(bf16[1,512,512]{2,1,0:T(8,128)(2,1)} %param.7), channel_id=1, source_target_pairs={{0,1},{1,2},{2,3},{3,4},{4,5},{5,6},{6,7},{7,8},{8,9},{9,10},{10,1... | collective-permute-start | bytes 1572872 | tf_op jit(solution)/shard_map/ppermute | solution.py:13
  10.8 15.1 %collective-permute-start.1 = (bf16[1,512,512]{2,1,0:T(8,128)(2,1)}, bf16[1,512,512]{2,1,0:T(8,128)(2,1)}, u32[]{:S(2)}, u32[]{:S(2)}) collective-permute-start(bf16[1,512,512]{2,1,0:T(8,128)(2,1)} %param.7), channel_id=1, source_target_pairs={{1,0},{2,1},{3,2},{4,3},{5,4},{6,5},{7,6},{8,7},{9,8},{10,9},{11,1... | collective-permute-start | bytes 1572872 | tf_op jit(solution)/shard_map/ppermute | solution.py:16
  12.1 15.1 %copy-start.3 = (s32[8]{0:T(128)S(1)}, s32[8]{0:T(128)}, u32[]{:S(2)}) copy-start(s32[8]{0:T(128)} %param.10) | copy-start | bytes 100
  58.7 1.0 copy-start.1
  59.7 103.0 %all-gather.3.cloned.1.call-start = ((), (), s32[]{:S(2)}) async-start(), calls=%async_computation.2 | async-start | bytes 1114112 | tf_op jit(solution)/shard_map/all_gather | solution.py:72
  127.1 60.8 %copy-start.2 = (bf16[32,512]{1,0:T(8,128)(2,1)}, bf16[32,512]{1,0:T(8,128)(2,1)S(1)}, u32[]{:S(2)}) copy-start(bf16[32,512]{1,0:T(8,128)(2,1)S(1)} %convert_element_type.14) | copy-start | bytes 98308
Sparse Core Ops, SparseCore 0:
  59.9 66.3 reduce-scatter.1
  128.3 34.3 all-gather.2
